TPU v7x, 128 devices: a whole 4x4x4 slice. The times are simulated.
128 devices in a mesh: cfg: 2 (over z_lo), seq: 8 (over x, core), blk: 8 (over z_hi, y).
Axes of the slice: x: 4, y: 4, z: 4 (z_hi: 2, z_lo: 2; z = z_hi * 2 + z_lo), core: 2. Of those that a mesh axis runs over, the one named last changes fastest.
Arguments:
- hidden: bfloat16 [2, 3072, 5120], P('cfg', 'seq', 'blk'), may hold values from -2.5 to 2.5
- modulation: float32 [3, 5120], replicated, may hold values from -4 to 4
- in_projection: bfloat16 [5120, 3, 3072], P(('cfg', 'seq'), None, 'blk'), may hold values from -0.078125 to 0.078125
- out_projection: bfloat16 [3072, 5120], P('blk', ('cfg', 'seq')), may hold values from -0.15625 to 0.15625
- lengths: int32 [5], replicated, may hold values from 1 to 1536, 3072 in all
- positions: int32 [3, 3072], P(None, 'seq'), may hold values from 0 to 63
- guidance: float32 [1], replicated, may hold values from 2 to 5
Outputs:
- guided: float32 [8, 2, 192, 5120], P('seq', 'cfg', None, 'blk')
Inputs may be any that keep to these rules, and one draw needn't show every extreme that they name: The clip lengths sum to 3072 and the longest is exactly 1536.
All inputs are finite; a program needn't handle non-finite values.
Results may differ from a plain program's by a relative error of at most 0.012.
The roundings to bfloat16 on the way count: a program that leaves them out, or rounds other values in their place, can miss the bound.
Values may be sent and summed in bfloat16 or wider, within the bound.
A program may use at most 128 MiB of HBM per device.

v0:
```python
import jax
import jax.numpy as jnp
import numpy as np
from jax import lax
from jax.sharding import Mesh, PartitionSpec as P

HEAD_DIM = 128
SEQ = ("x", "core")
BLK = ("zhi", "y")
SWAP = [(0, 1), (1, 0)]


def rotary_angles(head_width):
    third = head_width // 6
    first_dim = head_width - 4 * third
    other_dim = 2 * third
    pair_index = np.arange(head_width) // 2
    first_pairs = first_dim // 2
    other_pairs = other_dim // 2
    in_first = pair_index < first_pairs
    in_second = (pair_index >= first_pairs) & (pair_index < first_pairs + other_pairs)
    in_third = pair_index >= first_pairs + other_pairs
    row_first = np.where(in_first, 10000.0 ** (-2.0 * pair_index / first_dim), 0.0)
    row_second = np.where(
        in_second, 10000.0 ** (-2.0 * (pair_index - first_pairs) / other_dim), 0.0
    )
    row_third = np.where(
        in_third, 10000.0 ** (-2.0 * (pair_index - first_pairs - other_pairs) / other_dim), 0.0
    )
    return np.stack([row_first, row_second, row_third]).astype(np.float32)


def turn_matrix(head_width):
    row_index = np.arange(head_width)[:, None]
    col_index = np.arange(head_width)[None, :]
    upper = np.where((col_index == row_index + 1) & (row_index % 2 == 0), 1.0, 0.0)
    lower = np.where((col_index == row_index - 1) & (row_index % 2 == 1), -1.0, 0.0)
    return (upper + lower).astype(np.float32)


def layer_norm(inputs):
    row_mean = jnp.mean(inputs, -1, keepdims=True)
    centered = inputs - row_mean
    variance = jnp.mean(centered * centered, -1, keepdims=True)
    return centered * lax.rsqrt(variance + 1e-06)


def rms_norm(inputs):
    return inputs * lax.rsqrt(jnp.mean(inputs * inputs, -1, keepdims=True) + 1e-06)


def rotate(inputs, cosine, sine, turning):
    turned = jnp.einsum("thd,de->the", inputs, turning, precision=lax.Precision.HIGHEST)
    return inputs * cosine + turned * sine


def clip_of(clip_ends, token_index):
    return jnp.sum((token_index[:, None] >= clip_ends[None, :]).astype(jnp.int32), 1)


def local(hidden, modulation, in_projection, out_projection, lengths, positions, guidance):
    cfg = lax.axis_index("cfg")
    core = lax.axis_index("core")
    seq = lax.axis_index("x") * 2 + core
    states = hidden[0]
    tok_count = states.shape[0]
    half_rows = tok_count // 2
    n_blk = lax.axis_size(BLK)
    inner_width = in_projection.shape[2]
    head_count = inner_width // HEAD_DIM
    sent_rows = lax.dynamic_slice_in_dim(states, (1 - cfg) * half_rows, half_rows, 0)
    other_rows = lax.ppermute(sent_rows, "cfg", SWAP)
    mine_rows = lax.dynamic_slice_in_dim(states, cfg * half_rows, half_rows, 0)
    is_cond = cfg == 0
    cond_rows = jnp.where(is_cond, mine_rows, other_rows).astype(jnp.float32)
    uncond_rows = jnp.where(is_cond, other_rows, mine_rows).astype(jnp.float32)
    scale = guidance[0]
    hidden_part = uncond_rows + scale * (cond_rows - uncond_rows)
    full_states = lax.all_gather(states, BLK, axis=1, tiled=True)
    modulated = (
        layer_norm(full_states.astype(jnp.float32)) * (1.0 + modulation[1]) + modulation[0]
    ).astype(jnp.bfloat16)
    w_mine = lax.all_gather(in_projection, ("cfg", "x"), axis=0, tiled=True)
    w_other = lax.ppermute(w_mine, "core", SWAP)
    rows = in_projection.shape[0]
    n_pairs = w_mine.shape[0] // rows
    mod4 = modulated.reshape(tok_count, n_pairs, 2, rows)
    mod_mine = lax.dynamic_index_in_dim(mod4, core, axis=2, keepdims=False)
    mod_other = lax.dynamic_index_in_dim(mod4, 1 - core, axis=2, keepdims=False)
    mixed = jnp.einsum(
        "tjd,jdqe->tqe",
        mod_mine,
        w_mine.reshape(n_pairs, rows, 3, inner_width),
        preferred_element_type=jnp.float32,
    ) + jnp.einsum(
        "tjd,jdqe->tqe",
        mod_other,
        w_other.reshape(n_pairs, rows, 3, inner_width),
        preferred_element_type=jnp.float32,
    )
    mixed = mixed.reshape(tok_count, 3, head_count, HEAD_DIM)
    angle_table = jnp.asarray(rotary_angles(HEAD_DIM))
    turning = jnp.asarray(turn_matrix(HEAD_DIM))
    angles = jnp.einsum(
        "at,ae->te", positions.astype(jnp.float32), angle_table, precision=lax.Precision.HIGHEST
    )
    cosine = jnp.cos(angles)[:, None, :]
    sine = jnp.sin(angles)[:, None, :]
    queries = rotate(rms_norm(mixed[:, 0]), cosine, sine, turning).astype(jnp.bfloat16)
    key_rows = rotate(rms_norm(mixed[:, 1]), cosine, sine, turning).astype(jnp.bfloat16)
    value_rows = mixed[:, 2].astype(jnp.bfloat16)
    kv = jnp.stack([key_rows, value_rows], axis=1)
    kv_mine = lax.all_gather(kv, "x", axis=0, tiled=True)
    kv_other = lax.ppermute(kv_mine, "core", SWAP)
    kv_all = jnp.concatenate([kv_mine, kv_other], axis=0)
    key_piece = kv_all[:, 0]
    value_piece = kv_all[:, 1]
    row_count = key_piece.shape[0]
    n_x = kv_mine.shape[0] // tok_count
    clip_ends = jnp.cumsum(lengths)
    query_clip = clip_of(clip_ends, seq * tok_count + jnp.arange(tok_count, dtype=jnp.int32))
    key_row = jnp.arange(row_count, dtype=jnp.int32)
    key_block = key_row // tok_count
    key_core = jnp.where(key_block < n_x, core, 1 - core)
    key_token = (key_block % n_x * 2 + key_core) * tok_count + key_row % tok_count
    key_clip_all = clip_of(clip_ends, key_token)
    score_scale = HEAD_DIM ** (-0.5)
    start_state = (
        jnp.zeros((tok_count, head_count, HEAD_DIM), jnp.float32),
        jnp.zeros((head_count, tok_count), jnp.float32),
    )
    key_block_size = 512 if row_count % 512 == 0 else row_count

    def key_step(block_index, running):
        numerator, denominator = running
        key_slab = lax.dynamic_slice_in_dim(
            key_piece, block_index * key_block_size, key_block_size, 0
        )
        value_slab = lax.dynamic_slice_in_dim(
            value_piece, block_index * key_block_size, key_block_size, 0
        )
        key_clip = lax.dynamic_slice_in_dim(
            key_clip_all, block_index * key_block_size, key_block_size, 0
        )
        scores = (
            jnp.einsum("qhd,khd->hqk", queries, key_slab, preferred_element_type=jnp.float32)
            * score_scale
        )
        same_clip = query_clip[:, None] == key_clip[None, :]
        weights = jnp.where(same_clip[None], jnp.exp(scores), 0.0)
        numerator = numerator + jnp.einsum(
            "hqk,khd->qhd",
            weights.astype(jnp.bfloat16),
            value_slab,
            preferred_element_type=jnp.float32,
        )
        denominator = denominator + jnp.sum(weights, -1)
        return (numerator, denominator)

    numerator, denominator = lax.fori_loop(0, row_count // key_block_size, key_step, start_state)
    attended = (
        (numerator / jnp.transpose(denominator)[:, :, None])
        .astype(jnp.bfloat16)
        .reshape(tok_count, inner_width)
    )
    wo_mine = lax.all_gather(out_projection, ("cfg", "x"), axis=1, tiled=True)
    wo_other = lax.ppermute(wo_mine, "core", SWAP)
    cols = out_projection.shape[1]
    wo_mine = wo_mine.reshape(inner_width, n_blk, cols)
    wo_other = wo_other.reshape(inner_width, n_blk, cols)
    first_core = core == 0
    wo_full = jnp.stack(
        [jnp.where(first_core, wo_mine, wo_other), jnp.where(first_core, wo_other, wo_mine)], axis=2
    ).reshape(inner_width, n_blk, 2 * cols)
    weight = jnp.where(is_cond, scale, 1.0 - scale)
    gate = modulation[2].reshape(n_blk, 2 * cols) * weight
    partial = (
        jnp.einsum(
            "rte,ebn->rbtn",
            attended.reshape(2, half_rows, inner_width),
            wo_full,
            preferred_element_type=jnp.float32,
        )
        * gate[None, :, None, :]
    )
    projected = lax.psum_scatter(
        partial.reshape(2 * n_blk, half_rows, 2 * cols),
        ("cfg",) + BLK,
        scatter_dimension=0,
        tiled=True,
    )
    guided = hidden_part + projected[0]
    return guided.reshape(1, 1, half_rows, 2 * cols)


def solution(mesh):
    devices = mesh.devices.reshape(2, 4, 2, 2, 4)
    own = Mesh(devices, ("cfg", "x", "core", "zhi", "y"))
    return jax.shard_map(
        local,
        mesh=own,
        in_specs=(
            P("cfg", SEQ, BLK),
            P(),
            P(("cfg",) + SEQ, None, BLK),
            P(BLK, ("cfg",) + SEQ),
            P(),
            P(None, SEQ),
            P(),
        ),
        out_specs=P(SEQ, "cfg", None, BLK),
        check_vma=False,
    )
```

profile of v0, /device:TPU:0, one launch (start us, length us, event | category | flops | bytes accessed | tf_op | source)
XLA Modules:
  0.0 382.0 jit_solution(14357220380822101249)
XLA Ops:
  6.5 0.7 all-gather.8.cloned.1.call-update
  7.3 2.0 copy.34
  9.4 70.6 %all-gather.8.cloned.1.call-done = bf16[2560,3,384]{2,0,1:T(8,128)(2,1)} async-done(((bf16[320,3,384]{2,0,1:T(8,128)(2,1)}), bf16[2560,3,384]{2,0,1:T(8,128)(2,1)}) %all-gather.8.cloned.1.call-update) | async-done | bytes 5898256 | tf_op jit(solution)/shard_map/all_gather | solution.py:83
  80.8 1.8 cosine_bitcast_fusion
  82.8 1.1 slice_add_fusion
  84.0 66.6 %all-gather.12.cloned.1.call-done = bf16[1,384,5120]{1,2,0:T(8,128)(2,1)} async-done(((bf16[1,384,640]{1,2,0:T(8,128)(2,1)}), bf16[1,384,5120]{1,2,0:T(8,128)(2,1)}) %all-gather.12.cloned.1.call-update) | async-done | bytes 3932176 | tf_op jit(solution)/shard_map/all_gather | solution.py:79
  150.6 3.0 convert_reduce_fusion
  153.9 1.1 fusion.17
  155.0 2.9 fusion.20
  158.0 3.3 fusion.23
  161.3 6.0 %bitcast_add_fusion = f32[384,3,384]{0,2,1:T(8,128)S(1)} fusion(f32[384,3,384,1]{0,2,3,1:T(8,128)S(1)} %fusion.23, bf16[8,320,3,384]{3,1,0,2:T(8,128)(2,1)} %bitcast.18, bf16[384,8,2,320]{0,3,2,1:T(8,128)(2,1)S(1)} %bitcast.133, s32[]{:T(128)S(6)} %select_n.127), kind=kOutput, calls=%fused_computation.38 | convolution fusion | flops 2265366528 | bytes 11403268 | tf_op jit(solution)/shard_map/tjd,jdqe->tqe/dot_general | solution.py:95
  167.4 1.0 fusion.59
  169.8 0.9 pad_maximum_fusion.1
  170.7 20.4 %all-gather.6.cloned.1.call-done = bf16[384,2560]{0,1:T(8,128)(2,1)} async-done(((bf16[384,320]{0,1:T(8,128)(2,1)}), bf16[384,2560]{0,1:T(8,128)(2,1)}) %all-gather.6.cloned.1.call-update) | async-done | bytes 1966096 | tf_op jit(solution)/shard_map/all_gather | solution.py:166
  191.9 33.0 %all-gather.10.cloned.1.call-done = bf16[1536,2,3,128]{3,0,2,1:T(8,128)(2,1)} async-done(((bf16[384,2,3,128]{3,0,2,1:T(8,128)(2,1)}), bf16[1536,2,3,128]{3,0,2,1:T(8,128)(2,1)}) %all-gather.10.cloned.1.call-update) | async-done | bytes 2359312 | tf_op jit(solution)/shard_map/all_gather | solution.py:113
  225.7 1.9 broadcast_select_fusion.1
  227.6 2.3 pad_maximum_fusion
  229.9 1.3 copy.54
  231.5 2.5 fusion.32
  234.1 2.0 constant_dynamic-update-slice_fusion
  236.1 2.5 slice_bitcast_fusion
  238.6 26.7 %while.16 = (s32[]{:T(128)}, f32[384,3,128]{0,2,1:T(8,128)S(1)}, f32[3,384]{1,0:T(4,128)S(1)}, bf16[3072,3,128]{2,0,1:T(8,128)(2,1)}, s32[384]{0:T(512)S(1)}, /*...) while((s32[]{:T(128)}, f32[384,3,128]{0,2,1:T(8,128)S(1)}, ...), condition=%wide.region_9.10_spmd.clone, body=%wide.region_7.9_spmd.clone.sunk | while | flops 306021504 | bytes 7595706 | solution.py:160
  238.6 0.8 dynamic_slice.70
  239.5 1.7 fusion.77
  241.2 1.7 fusion.78
  243.0 0.8 dynamic_slice.70
  244.0 1.7 fusion.77
  245.7 1.7 fusion.78
  247.5 0.8 dynamic_slice.70
  248.4 1.7 fusion.77
  250.2 1.7 fusion.78
  251.9 0.8 dynamic_slice.70
  252.9 1.7 fusion.77
  254.6 1.7 fusion.78
  256.4 0.8 dynamic_slice.70
  257.3 1.7 fusion.77
  259.0 1.7 fusion.78
  260.8 0.8 dynamic_slice.70
  261.7 1.7 fusion.77
  263.5 1.7 fusion.78
  265.5 0.8 copy.50
  266.3 4.3 %multiply_bitcast_fusion = f32[2,8,192,640]{3,2,0,1:T(8,128)S(1)} fusion(f32[8,640]{1,0:T(8,128)S(1)} %copy-done.5, bf16[384,8,640,1]{0,2,3,1:T(8,128)(2,1)} %bitcast.129, bf16[2,192,384]{2,1,0:T(8,128)(2,1)S(1)} %copy.50), kind=kOutput, calls=%fused_computation.26 | convolution fusion | flops 1511915520 | bytes 12111872 | tf_op jit(solution)/shard_map/rte,ebn->rbtn/dot_general | solution.py:178
  270.7 3.6 copy.43
  274.3 1.0 copy-done.2
  275.3 1.6 collective-permute-start
  276.9 6.8 %collective-permute-done = bf16[192,640]{1,0:T(8,128)(2,1)S(1)} collective-permute-done((bf16[192,640]{1,0:T(8,128)(2,1)S(1)}, bf16[192,640]{1,0:T(8,128)(2,1)S(1)}, u32[]{:S(2)}, u32[]{:S(2)}) %collective-permute-start) | collective-permute-done | bytes 245792 | tf_op jit(solution)/shard_map/ppermute | solution.py:72
  283.7 89.8 %reduce-scatter.2.cloned.1.call-done = f32[1,192,640]{2,1,0:T(8,128)} async-done(((f32[16,192,640]{2,1,0:T(8,128)}), f32[1,192,640]{2,1,0:T(8,128)}) %reduce-scatter.2.cloned.1.call-update) | async-done | bytes 491536 | tf_op jit(solution)/shard_map/reduce_scatter | solution.py:186
  373.6 1.9 fusion.38
  (73 shorter events, 5.7 us)
Async XLA Ops:
  6.5 73.5 %all-gather.8.cloned.1.call-start = ((), (), s32[]{:S(2)}) async-start(), calls=%async_computation.2 | async-start | bytes 6635520 | tf_op jit(solution)/shard_map/all_gather | solution.py:83
  7.3 143.4 %all-gather.12.cloned.1.call-start = ((), (), s32[]{:S(2)}) async-start(), calls=%async_computation.5 | async-start | bytes 4423680 | tf_op jit(solution)/shard_map/all_gather | solution.py:79
  9.3 181.8 %all-gather.6.cloned.1.call-start = ((), (), s32[]{:S(2)}) async-start(), calls=%async_computation.1 | async-start | bytes 2211840 | tf_op jit(solution)/shard_map/all_gather | solution.py:166
  80.0 81.2 %collective-permute-start.2 = (bf16[2560,3,384]{2,0,1:T(8,128)(2,1)}, bf16[2560,3,384]{2,0,1:T(8,128)(2,1)}, u32[]{:S(2)}, u32[]{:S(2)}) collective-permute-start(bf16[2560,3,384]{2,0,1:T(8,128)(2,1)} %all-gather.8.cloned.1.call-done), channel_id=1, source_target_pairs={{0,8},{8,0},{1,9},{9,1},{2,10},{10,2},{3,11},{11,3},{4,12},{12,4},... | collective-permute-start | bytes 17694728 | tf_op jit(solution)/shard_map/ppermute | solution.py:84
  80.1 144.8 %all-gather.10.cloned.1.call-start = ((), (), s32[]{:S(2)}) async-start(), calls=%async_computation.3 | async-start | bytes 2949120 | tf_op jit(solution)/shard_map/all_gather | solution.py:113
  82.7 86.4 %copy-start.3 = (f32[384,128]{1,0:T(8,128)}, f32[384,128]{1,0:T(8,128)S(1)}, u32[]{:S(2)}) copy-start(f32[384,128]{1,0:T(8,128)S(1)} %copy.36) | copy-start | bytes 589828
  82.8 86.2 %copy-start.4 = (f32[384,128]{1,0:T(8,128)}, f32[384,128]{1,0:T(8,128)S(1)}, u32[]{:S(2)}) copy-start(f32[384,128]{1,0:T(8,128)S(1)} %copy.37) | copy-start | bytes 589828
  150.6 3.3 copy-start
  153.9 4.0 %slice-start = ((s8[5898240]{0:T(1024)(128)(4,1)}), s8[4194304]{0:T(1024)(128)(4,1)S(1)}, s32[]{:S(2)}) async-start(s8[5898240]{0:T(1024)(128)(4,1)} %bitcast.141), calls=%async_computation.6 | async-start | bytes 8388608
  155.0 2.9 slice-start.1
  167.3 1.8 copy-start.7
  167.4 23.8 %copy-start.8 = (s32[5]{0:T(128)S(1)}, s32[5]{0:T(128)}, u32[]{:S(2)}) copy-start(s32[5]{0:T(128)} %param.15) | copy-start | bytes 64
  170.7 202.9 %reduce-scatter.2.cloned.1.call-start = ((), (), s32[]{:S(2)}) async-start(), calls=%async_computation.4 | async-start | bytes 8355840 | tf_op jit(solution)/shard_map/reduce_scatter | solution.py:186
  191.1 34.6 %collective-permute-start.1 = (bf16[384,2560]{0,1:T(8,128)(2,1)}, bf16[384,2560]{0,1:T(8,128)(2,1)S(1)}, u32[]{:S(2)}, u32[]{:S(2)}) collective-permute-start(bf16[384,2560]{0,1:T(8,128)(2,1)} %all-gather.6.cloned.1.call-done), channel_id=1, source_target_pairs={{0,8},{8,0},{1,9},{9,1},{2,10},{10,2},{3,11},{11,3},{4,12},{12,4},... | collective-permute-start | bytes 5898248 | tf_op jit(solution)/shard_map/ppermute | solution.py:167
  224.9 9.2 %collective-permute-start.3 = (bf16[1536,2,3,128]{3,0,2,1:T(8,128)(2,1)}, bf16[1536,2,3,128]{3,0,2,1:T(8,128)(2,1)}, u32[]{:S(2)}, u32[]{:S(2)}) collective-permute-start(bf16[1536,2,3,128]{3,0,2,1:T(8,128)(2,1)} %all-gather.10.cloned.1.call-done), channel_id=1, source_target_pairs={{0,8},{8,0},{1,9},{9,1},{2,10},{10,2},{3,11},{11,3},{4,12},{12,4},... | collective-permute-start | bytes 7077896 | tf_op jit(solution)/shard_map/ppermute | solution.py:114
  227.6 6.3 %copy-start.1 = (bf16[1536,2,3,128]{3,0,2,1:T(8,128)(2,1)S(1)}, bf16[1536,2,3,128]{3,0,2,1:T(8,128)(2,1)}, u32[]{:S(2)}) copy-start(bf16[1536,2,3,128]{3,0,2,1:T(8,128)(2,1)} %all-gather.10.cloned.1.call-done) | copy-start | bytes 7077892
  236.1 2.5 copy-start.6
  238.6 27.7 %copy-start.5 = (f32[8,640]{1,0:T(8,128)S(1)}, f32[8,640]{1,0:T(8,128)}, u32[]{:S(2)}) copy-start(f32[8,640]{1,0:T(8,128)} %mul.177) | copy-start | bytes 61444
  274.2 1.0 copy-start.2
  275.3 8.4 %collective-permute-start = (bf16[192,640]{1,0:T(8,128)(2,1)S(1)}, bf16[192,640]{1,0:T(8,128)(2,1)S(1)}, u32[]{:S(2)}, u32[]{:S(2)}) collective-permute-start(bf16[192,640]{1,0:T(8,128)(2,1)S(1)} %dynamic-slice_bitcast_fusion), channel_id=1, source_target_pairs={{0,64},{64,0},{1,65},{65,1},{2,66},{66,2},{3,67},{67,3},{4,68},{68... | collective-permute-start | bytes 737288 | tf_op jit(solution)/shard_map/ppermute | solution.py:72
Sparse Core Ops, SparseCore 0:
  9.0 71.0 all-gather.7
  82.4 68.2 all-gather.11
  152.3 38.7 all-gather.5
  192.6 32.2 all-gather.9
  274.4 99.1 reduce-scatter.1
where the time goes:
time: 383 us; the launch traced here: 382 us
  waiting for transfers between devices  288 us (75%)
  matrix products  39.3 us (10%)
  local copies, waits for them, and re-layouts  20.7 us (5%)
  other arithmetic  17.8 us (5%)
  between operations  14.1 us (4%)
    reduce_scatter x1, waiting for transfers between devices, local(): lax.psum_scatter(partial.reshape(2 * n_blk, half_rows, 2 * cols), ('cfg',...  89.8 us
    all_gather x1, waiting for transfers between devices, local(): w_mine = lax.all_gather(in_projection, ('cfg', 'x'), axis=0, tiled=True)  70.6 us
    all_gather x1, waiting for transfers between devices, local(): full_states = lax.all_gather(states, BLK, axis=1, tiled=True)  66.6 us
    all_gather x1, waiting for transfers between devices, local(): kv_mine = lax.all_gather(kv, 'x', axis=0, tiled=True)  33 us
    all_gather x1, waiting for transfers between devices, local(): wo_mine = lax.all_gather(out_projection, ('cfg', 'x'), axis=1, tiled=True)  20.4 us
    dot_general x6, matrix products, key_step(): jnp.einsum('qhd,khd->hqk', queries, key_slab, preferred_element_type=jnp....  10.4 us
    dot_general x6, matrix products, key_step(): jnp.einsum('hqk,khd->qhd', weights.astype(jnp.bfloat16), value_slab, pref...  10.4 us
  transfers between devices with their start and end apart: 9, of which 6 were waited for; matrix products, arithmetic and copies ran while one was open for 9% of the time, Pallas kernels for 0%

commit v1 on v0

--- a/solution.py
+++ b/solution.py
@@ -80,7 +80,12 @@
     modulated = (
         layer_norm(full_states.astype(jnp.float32)) * (1.0 + modulation[1]) + modulation[0]
     ).astype(jnp.bfloat16)
-    w_mine = lax.all_gather(in_projection, ("cfg", "x"), axis=0, tiled=True)
+    w_mine = jnp.concatenate(
+        lax.all_to_all(
+            jnp.stack([in_projection] * lax.axis_size(("cfg", "x"))), ("cfg", "x"), 0, 0
+        ),
+        axis=0,
+    )
     w_other = lax.ppermute(w_mine, "core", SWAP)
     rows = in_projection.shape[0]
     n_pairs = w_mine.shape[0] // rows

time: 383 us -> 370 us (0.966)
  waiting for transfers between devices: 288 us -> 259 us
  local copies, waits for them, and re-layouts: 20.7 us -> 30.1 us
  starting transfers between devices: 1.81 us -> 7.69 us
    all_gather x1 -> x0, waiting for transfers between devices: 70.6 us -> none  [local(): w_mine = lax.all_gather(in_projection, ('cfg', 'x'), axis=0, tiled=True)]
    all_to_all x0 -> x1, waiting for transfers between devices: none -> 66.6 us  [local(): lax.all_to_all(jnp.stack([in_projection] * lax.axis_size(('cfg', 'x'))),...]
    all_gather x1, waiting for transfers between devices: 66.6 us -> 44.6 us  [local(): full_states = lax.all_gather(states, BLK, axis=1, tiled=True)]
    all_to_all x0 -> x1, local copies, waits for them, and re-layouts: none -> 5.9 us  [local(): lax.all_to_all(jnp.stack([in_projection] * lax.axis_size(('cfg', 'x'))),...]
    all_to_all x0 -> x1, starting transfers between devices: none -> 5.9 us  [local(): lax.all_to_all(jnp.stack([in_projection] * lax.axis_size(('cfg', 'x'))),...]
    another operation x0 -> x1, local copies, waits for them, and re-layouts: none -> 4.53 us  [local(): jnp.stack([in_projection] * lax.axis_size(('cfg', 'x')))]
  transfers between devices with their start and end apart: 9 -> 9, of which waited for: 6 -> 6; matrix products, arithmetic and copies ran while one was open for 9% -> 11% of each run, Pallas kernels for 0% -> 0%
where the time goes in v1:
time: 370 us; the launch traced here: 369 us
  waiting for transfers between devices  259 us (70%)
  matrix products  41.4 us (11%)
  local copies, waits for them, and re-layouts  30.1 us (8%)
  other arithmetic  16.8 us (5%)
  between operations  14.1 us (4%)
  starting transfers between devices  7.69 us (2%)
    reduce_scatter x1, waiting for transfers between devices, local(): lax.psum_scatter(partial.reshape(2 * n_blk, half_rows, 2 * cols), ('cfg',...  90 us
    all_to_all x1, waiting for transfers between devices, local(): lax.all_to_all(jnp.stack([in_projection] * lax.axis_size(('cfg', 'x'))),...  66.6 us
    all_gather x1, waiting for transfers between devices, local(): full_states = lax.all_gather(states, BLK, axis=1, tiled=True)  44.6 us
    all_gather x1, waiting for transfers between devices, local(): kv_mine = lax.all_gather(kv, 'x', axis=0, tiled=True)  33.1 us
    all_gather x1, waiting for transfers between devices, local(): wo_mine = lax.all_gather(out_projection, ('cfg', 'x'), axis=1, tiled=True)  17.6 us
    dot_general x6, matrix products, key_step(): jnp.einsum('qhd,khd->hqk', queries, key_slab, preferred_element_type=jnp....  10.4 us
    dot_general x6, matrix products, key_step(): jnp.einsum('hqk,khd->qhd', weights.astype(jnp.bfloat16), value_slab, pref...  10.4 us
  transfers between devices with their start and end apart: 9, of which 6 were waited for; matrix products, arithmetic and copies ran while one was open for 11% of the time, Pallas kernels for 0%

profile of v1, /device:TPU:0, one launch (start us, length us, event | category | flops | bytes accessed | tf_op | source)
XLA Modules:
  0.0 369.2 jit_solution(17632639510671701647)
XLA Ops:
  6.5 4.5 %stack.9 = bf16[8,320,3,384]{3,1,2,0:T(8,128)(2,1)} broadcast(bf16[320,3,384]{2,0,1:T(8,128)(2,1)} %param.13), dimensions={1,2,3} | broadcast | bytes 6635520 | tf_op jit(solution)/shard_map/stack | solution.py:85
  11.1 5.9 %all-to-all-start = ((bf16[8,320,3,384]{3,1,2,0:T(8,128)(2,1)}), bf16[8,320,3,384]{3,1,2,0:T(8,128)(2,1)}, u32[]{:S(2)}, u32[]{:S(2)}) async-start(bf16[8,320,3,384]{3,1,2,0:T(8,128)(2,1)} %stack.9), calls=%async_computation | async-start | bytes 11796480 | tf_op jit(solution)/shard_map/all_to_all | solution.py:84
  17.0 1.0 copy.59
  18.1 66.6 %all-to-all-done = bf16[8,320,3,384]{3,1,2,0:T(8,128)(2,1)} async-done(((bf16[8,320,3,384]{3,1,2,0:T(8,128)(2,1)}), bf16[8,320,3,384]{3,1,2,0:T(8,128)(2,1)}, u32[]{:S(2)}, u32[]{:S(2)}) %all-to-all-start) | async-done | bytes 5898272 | tf_op jit(solution)/shard_map/all_to_all | solution.py:84
  84.7 5.9 %copy.60 = bf16[8,320,3,384]{3,1,0,2:T(8,128)(2,1)} copy(bf16[8,320,3,384]{3,1,2,0:T(8,128)(2,1)} %all-to-all-done) | data formatting | bytes 11796480 | tf_op jit(solution)/shard_map/all_to_all | solution.py:84
  91.4 1.1 cosine_bitcast_fusion
  92.9 44.6 %all-gather.9.cloned.1.call-done = bf16[1,384,5120]{1,2,0:T(8,128)(2,1)} async-done(((bf16[1,384,640]{1,2,0:T(8,128)(2,1)}), bf16[1,384,5120]{1,2,0:T(8,128)(2,1)}) %all-gather.9.cloned.1.call-update) | async-done | bytes 3932176 | tf_op jit(solution)/shard_map/all_gather | solution.py:79
  137.4 3.0 convert_reduce_fusion
  140.7 1.1 fusion.17
  141.8 2.9 fusion.20
  144.8 6.0 %fusion.21 = f32[384,3,384,1]{0,2,1,3:T(8,128)S(1)} fusion(bf16[8,320,3,384]{3,1,2,0:T(8,128)(2,1)} %all-to-all-done, bf16[384,8,2,320]{0,3,2,1:T(8,128)(2,1)S(1)} %bitcast.136, s32[]{:T(128)S(6)} %select_n.126), kind=kOutput, calls=%fused_computation.30 | convolution fusion | flops 2264924160 | bytes 9633796 | tf_op jit(solution)/shard_map/tjd,jdqe->tqe/dot_general | solution.py:95
  150.8 6.1 %bitcast_add_fusion = f32[384,3,384]{0,2,1:T(8,128)S(1)} fusion(f32[384,3,384,1]{0,2,1,3:T(8,128)S(1)} %fusion.21, bf16[8,320,3,384]{3,1,0,2:T(8,128)(2,1)} %bitcast.18, bf16[384,8,2,320]{0,3,2,1:T(8,128)(2,1)S(1)} %bitcast.137, s32[]{:T(128)S(6)} %select_n.127), kind=kOutput, calls=%fused_computation.38 | convolution fusion | flops 2265366528 | bytes 11403268 | tf_op jit(solution)/shard_map/tjd,jdqe->tqe/dot_general | solution.py:100
  156.9 1.0 fusion.59
  159.3 0.9 pad_maximum_fusion.1
  160.3 17.6 %all-gather.5.cloned.1.call-done = bf16[384,2560]{0,1:T(8,128)(2,1)} async-done(((bf16[384,320]{0,1:T(8,128)(2,1)}), bf16[384,2560]{0,1:T(8,128)(2,1)}) %all-gather.5.cloned.1.call-update) | async-done | bytes 1966096 | tf_op jit(solution)/shard_map/all_gather | solution.py:171
  178.7 33.1 %all-gather.7.cloned.1.call-done = bf16[1536,2,3,128]{3,0,2,1:T(8,128)(2,1)} async-done(((bf16[384,2,3,128]{3,0,2,1:T(8,128)(2,1)}), bf16[1536,2,3,128]{3,0,2,1:T(8,128)(2,1)}) %all-gather.7.cloned.1.call-update) | async-done | bytes 2359312 | tf_op jit(solution)/shard_map/all_gather | solution.py:118
  212.7 1.9 broadcast_select_fusion.1
  214.6 2.3 pad_maximum_fusion
  216.9 1.3 copy.81
  218.4 2.5 fusion.32
  221.1 2.0 constant_dynamic-update-slice_fusion
  223.0 2.5 slice_bitcast_fusion
  225.5 26.6 %while.16 = (s32[]{:T(128)}, f32[384,3,128]{0,2,1:T(8,128)S(1)}, f32[3,384]{1,0:T(4,128)S(1)}, bf16[3072,3,128]{2,0,1:T(8,128)(2,1)}, s32[384]{0:T(512)S(1)}, /*...) while((s32[]{:T(128)}, f32[384,3,128]{0,2,1:T(8,128)S(1)}, ...), condition=%wide.region_9.10_spmd.clone, body=%wide.region_7.9_spmd.clone.sunk | while | flops 306021504 | bytes 7595706 | solution.py:165
  225.5 0.8 dynamic_slice.70
  226.4 1.7 fusion.77
  228.2 1.7 fusion.78
  230.0 0.8 dynamic_slice.70
  230.9 1.7 fusion.77
  232.6 1.7 fusion.78
  234.4 0.8 dynamic_slice.70
  235.3 1.7 fusion.77
  237.1 1.7 fusion.78
  238.8 0.8 dynamic_slice.70
  239.8 1.7 fusion.77
  241.5 1.7 fusion.78
  243.3 0.7 dynamic_slice.70
  244.2 1.7 fusion.77
  246.0 1.7 fusion.78
  248.6 1.7 fusion.77
  250.4 1.7 fusion.78
  252.5 0.8 copy.77
  253.2 4.3 %multiply_bitcast_fusion = f32[2,8,192,640]{3,2,0,1:T(8,128)S(1)} fusion(f32[8,640]{1,0:T(8,128)S(1)} %copy-done.6, bf16[384,8,640,1]{0,2,3,1:T(8,128)(2,1)} %bitcast.133, bf16[2,192,384]{2,1,0:T(8,128)(2,1)S(1)} %copy.77), kind=kOutput, calls=%fused_computation.26 | convolution fusion | flops 1511915520 | bytes 12111872 | tf_op jit(solution)/shard_map/rte,ebn->rbtn/dot_general | solution.py:183
  257.6 3.6 copy.70
  261.2 1.0 copy-done.3
  262.2 1.6 collective-permute-start
  263.9 6.8 %collective-permute-done = bf16[192,640]{1,0:T(8,128)(2,1)S(1)} collective-permute-done((bf16[192,640]{1,0:T(8,128)(2,1)S(1)}, bf16[192,640]{1,0:T(8,128)(2,1)S(1)}, u32[]{:S(2)}, u32[]{:S(2)}) %collective-permute-start) | collective-permute-done | bytes 245792 | tf_op jit(solution)/shard_map/ppermute | solution.py:72
  270.7 90.0 %reduce-scatter.2.cloned.1.call-done = f32[1,192,640]{2,1,0:T(8,128)} async-done(((f32[16,192,640]{2,1,0:T(8,128)}), f32[1,192,640]{2,1,0:T(8,128)}) %reduce-scatter.2.cloned.1.call-update) | async-done | bytes 491536 | tf_op jit(solution)/shard_map/reduce_scatter | solution.py:191
  360.7 1.9 fusion.38
  (77 shorter events, 6.5 us)
Async XLA Ops:
  11.1 5.9 %copy-start.2 = (bf16[1,384,640]{2,1,0:T(8,128)(2,1)S(1)}, bf16[1,384,640]{2,1,0:T(8,128)(2,1)}, u32[]{:S(2)}) copy-start(bf16[1,384,640]{2,1,0:T(8,128)(2,1)} %param.11) | copy-start | bytes 1474564
  11.1 73.7 %all-to-all-start = ((bf16[8,320,3,384]{3,1,2,0:T(8,128)(2,1)}), bf16[8,320,3,384]{3,1,2,0:T(8,128)(2,1)}, u32[]{:S(2)}, u32[]{:S(2)}) async-start(bf16[8,320,3,384]{3,1,2,0:T(8,128)(2,1)} %stack.9), calls=%async_computation | async-start | bytes 11796480 | tf_op jit(solution)/shard_map/all_to_all | solution.py:84
  17.0 120.5 %all-gather.9.cloned.1.call-start = ((), (), s32[]{:S(2)}) async-start(), calls=%async_computation.5 | async-start | bytes 4423680 | tf_op jit(solution)/shard_map/all_gather | solution.py:79
  18.0 73.3 %copy-start.10 = (s32[3,384]{1,0:T(4,128)S(1)}, s32[3,384]{1,0:T(4,128)}, u32[]{:S(2)}) copy-start(s32[3,384]{1,0:T(4,128)} %param.16) | copy-start | bytes 13828
  18.1 73.3 %copy-start.11 = (f32[3,128]{1,0:T(4,128)S(1)}, f32[3,128]{1,0:T(4,128)}, u32[]{:S(2)}) copy-start(f32[3,128]{1,0:T(4,128)} %constant.129.clone) | copy-start | bytes 4612
  18.1 74.7 %copy-start.9 = (f32[3,5120]{1,0:T(4,128)S(1)}, f32[3,5120]{1,0:T(4,128)}, u32[]{:S(2)}) copy-start(f32[3,5120]{1,0:T(4,128)} %param.12) | copy-start | bytes 184324
  18.1 159.8 %all-gather.5.cloned.1.call-start = ((), (), s32[]{:S(2)}) async-start(), calls=%async_computation.2 | async-start | bytes 2211840 | tf_op jit(solution)/shard_map/all_gather | solution.py:171
  90.6 60.1 %collective-permute-start.2 = (bf16[2560,3,384]{2,0,1:T(8,128)(2,1)}, bf16[2560,3,384]{2,0,1:T(8,128)(2,1)}, u32[]{:S(2)}, u32[]{:S(2)}) collective-permute-start(bf16[2560,3,384]{2,0,1:T(8,128)(2,1)} %bitcast.17), channel_id=1, source_target_pairs={{0,8},{8,0},{1,9},{9,1},{2,10},{10,2},{3,11},{11,3},{4,12},{12,4},... | collective-permute-start | bytes 17694728 | tf_op jit(solution)/shard_map/ppermute | solution.py:89
  90.7 121.2 %all-gather.7.cloned.1.call-start = ((), (), s32[]{:S(2)}) async-start(), calls=%async_computation.3 | async-start | bytes 2949120 | tf_op jit(solution)/shard_map/all_gather | solution.py:118
  92.6 66.0 %copy-start.4 = (f32[384,128]{1,0:T(8,128)}, f32[384,128]{1,0:T(8,128)S(1)}, u32[]{:S(2)}) copy-start(f32[384,128]{1,0:T(8,128)S(1)} %copy.63) | copy-start | bytes 589828
  92.7 65.9 %copy-start.5 = (f32[384,128]{1,0:T(8,128)}, f32[384,128]{1,0:T(8,128)S(1)}, u32[]{:S(2)}) copy-start(f32[384,128]{1,0:T(8,128)S(1)} %copy.64) | copy-start | bytes 589828
  137.4 3.3 copy-start
  156.9 1.8 copy-start.8
  156.9 21.0 %copy-start.12 = (s32[5]{0:T(128)S(1)}, s32[5]{0:T(128)}, u32[]{:S(2)}) copy-start(s32[5]{0:T(128)} %param.15) | copy-start | bytes 64
  160.2 200.4 %reduce-scatter.2.cloned.1.call-start = ((), (), s32[]{:S(2)}) async-start(), calls=%async_computation.4 | async-start | bytes 8355840 | tf_op jit(solution)/shard_map/reduce_scatter | solution.py:191
  177.9 34.7 %collective-permute-start.1 = (bf16[384,2560]{0,1:T(8,128)(2,1)}, bf16[384,2560]{0,1:T(8,128)(2,1)S(1)}, u32[]{:S(2)}, u32[]{:S(2)}) collective-permute-start(bf16[384,2560]{0,1:T(8,128)(2,1)} %all-gather.5.cloned.1.call-done), channel_id=1, source_target_pairs={{0,8},{8,0},{1,9},{9,1},{2,10},{10,2},{3,11},{11,3},{4,12},{12,4},... | collective-permute-start | bytes 5898248 | tf_op jit(solution)/shard_map/ppermute | solution.py:172
  211.9 9.2 %collective-permute-start.3 = (bf16[1536,2,3,128]{3,0,2,1:T(8,128)(2,1)}, bf16[1536,2,3,128]{3,0,2,1:T(8,128)(2,1)}, u32[]{:S(2)}, u32[]{:S(2)}) collective-permute-start(bf16[1536,2,3,128]{3,0,2,1:T(8,128)(2,1)} %all-gather.7.cloned.1.call-done), channel_id=1, source_target_pairs={{0,8},{8,0},{1,9},{9,1},{2,10},{10,2},{3,11},{11,3},{4,12},{12,4},... | collective-permute-start | bytes 7077896 | tf_op jit(solution)/shard_map/ppermute | solution.py:119
  214.6 6.3 %copy-start.1 = (bf16[1536,2,3,128]{3,0,2,1:T(8,128)(2,1)S(1)}, bf16[1536,2,3,128]{3,0,2,1:T(8,128)(2,1)}, u32[]{:S(2)}) copy-start(bf16[1536,2,3,128]{3,0,2,1:T(8,128)(2,1)} %all-gather.7.cloned.1.call-done) | copy-start | bytes 7077892
  223.0 2.5 copy-start.7
  225.5 27.7 %copy-start.6 = (f32[8,640]{1,0:T(8,128)S(1)}, f32[8,640]{1,0:T(8,128)}, u32[]{:S(2)}) copy-start(f32[8,640]{1,0:T(8,128)} %mul.177) | copy-start | bytes 61444
  261.2 1.0 copy-start.3
  262.2 8.5 %collective-permute-start = (bf16[192,640]{1,0:T(8,128)(2,1)S(1)}, bf16[192,640]{1,0:T(8,128)(2,1)S(1)}, u32[]{:S(2)}, u32[]{:S(2)}) collective-permute-start(bf16[192,640]{1,0:T(8,128)(2,1)S(1)} %dynamic-slice_bitcast_fusion), channel_id=1, source_target_pairs={{0,64},{64,0},{1,65},{65,1},{2,66},{66,2},{3,67},{67,3},{4,68},{68... | collective-permute-start | bytes 737288 | tf_op jit(solution)/shard_map/ppermute | solution.py:72
Sparse Core Ops, SparseCore 0:
  20.1 117.2 all-gather.8
  139.1 38.7 all-gather.4
  179.6 32.2 all-gather.6
  261.3 99.3 reduce-scatter.1
